TPU v7x, 32 devices: a whole 2x2x4 slice. The times are simulated.
32 devices in a mesh: slab: 4 (over x, core), kt: 8 (over z, y).
Axes of the slice: x: 2, y: 2, z: 4, core: 2. Of those that a mesh axis runs over, the one named last changes fastest.
Arguments:
- energies: float32 [4], replicated, may hold values from -0.5 to 0.1
- onsite: float32 [8, 4, 384], P('kt', 'slab'), may hold values from -3.5 to -2.5
- hamiltonian: bfloat16 [8, 4, 2, 384, 384], P('kt', 'slab'), may hold values from -0.109375 to 0.109375
- hopping: bfloat16 [8, 4, 2, 384, 384], P('kt', 'slab'), may hold values from -0.15625 to 0.15625
- contact: bfloat16 [8, 2, 384, 384], P('kt'), may hold values from -2 to 2
- previous: bfloat16 [8, 4, 4, 2, 2, 384, 384], P('kt', None, 'slab'), may hold values from -4 to 4
- neighbours: int32 [8, 2], P('kt'), may hold values from 0 to 7, as said below
- mode_index: int32 [8, 2], P('kt'), may hold values from 0 to 3
- mode_strength: float32 [4], replicated, may hold values from 0.25 to 1
Outputs:
- retarded: bfloat16 [8, 4, 4, 2, 384, 384], P('kt', None, 'slab')
- lesser: bfloat16 [8, 4, 4, 2, 384, 384], P('kt', None, 'slab')
Inputs may be any that keep to these rules, and one draw needn't show every extreme that they name: neighbours[k, 0] is k - 1 or k - 2 and neighbours[k, 1] is k + 1 or k + 2, modulo 8.
All inputs are finite; a program needn't handle non-finite values.
Results may differ from a plain program's by a relative error of at most 0.017.
Values may be sent and summed in bfloat16 or wider, within the bound.
A program may use at most 128 MiB of HBM per device.

v0:
```python
import jax
import jax.numpy as jnp
from jax import lax
from jax.sharding import PartitionSpec as P

broaden = 0.05
fermi_level = 0.0
thermal = 0.1


def from_behind(value, axis, by):
    peers = lax.axis_size(axis)
    return lax.ppermute(value, axis, [(i, (i + by) % peers) for i in range(peers)])


def as_sent(value):
    return jax.tree.map(lambda a: a.astype(jnp.bfloat16) if a.dtype == jnp.float32 else a, value)


def combine(pieces):
    real_part = pieces[..., 0, 0, :, :] - pieces[..., 1, 1, :, :]
    imaginary_part = pieces[..., 0, 1, :, :] + pieces[..., 1, 0, :, :]
    return jnp.stack([real_part, imaginary_part], axis=-3)


def complex_mul(first_op, second_op):
    return combine(
        jnp.einsum("pij,qjk->pqik", first_op, second_op, preferred_element_type=jnp.float32)
    )


def adjoint(matrix):
    return jnp.stack([matrix[0].T, -matrix[1].T])


def mul_adjoint(first_op, second_op):
    pieces = jnp.einsum(
        "...pij,qkj->...pqik", first_op, second_op, preferred_element_type=jnp.float32
    )
    real_part = pieces[..., 0, 0, :, :] + pieces[..., 1, 1, :, :]
    imaginary_part = pieces[..., 1, 0, :, :] - pieces[..., 0, 1, :, :]
    return jnp.stack([real_part, imaginary_part], axis=-3)


def slab_update(boundary, energy, levels, hamilton, coupling, phonon):
    moved_blocks = combine(
        jnp.einsum("pij,sqjk->spqik", coupling, boundary, preferred_element_type=jnp.float32)
    ).astype(jnp.bfloat16)
    self_both = mul_adjoint(moved_blocks, coupling)
    self_retarded = self_both[0]
    self_lesser = self_both[1]
    size = levels.shape[0]
    on_diagonal = lax.broadcasted_iota(jnp.int32, (size, size), 0) == lax.broadcasted_iota(
        jnp.int32, (size, size), 1
    )
    system_real = (
        jnp.where(on_diagonal, (energy - levels)[:, None], 0.0)
        - hamilton[0].astype(jnp.float32)
        - self_retarded[0]
        - phonon[0, 0]
    )
    system_imaginary = (
        jnp.where(on_diagonal, broaden, 0.0)
        - hamilton[1].astype(jnp.float32)
        - self_retarded[1]
        - phonon[0, 1]
    )
    diagonal_real = jnp.sum(jnp.where(on_diagonal, system_real, 0.0), axis=1)
    diagonal_imaginary = jnp.sum(jnp.where(on_diagonal, system_imaginary, 0.0), axis=1)
    modulus = diagonal_real * diagonal_real + diagonal_imaginary * diagonal_imaginary
    inverse_real = diagonal_real / modulus
    inverse_imaginary = -diagonal_imaginary / modulus
    scaled_real = (
        inverse_real[:, None] * system_real - inverse_imaginary[:, None] * system_imaginary
    )
    scaled_imaginary = (
        inverse_real[:, None] * system_imaginary + inverse_imaginary[:, None] * system_real
    )
    sandwich_real = (
        scaled_real * inverse_real[None, :] - scaled_imaginary * inverse_imaginary[None, :]
    )
    sandwich_imaginary = (
        scaled_real * inverse_imaginary[None, :] + scaled_imaginary * inverse_real[None, :]
    )
    first_guess = jnp.stack(
        [
            jnp.where(on_diagonal, 2.0 * inverse_real[:, None], 0.0) - sandwich_real,
            jnp.where(on_diagonal, 2.0 * inverse_imaginary[:, None], 0.0) - sandwich_imaginary,
        ]
    )
    first_rounded = first_guess.astype(jnp.bfloat16)
    system_rounded = jnp.stack([system_real, system_imaginary]).astype(jnp.bfloat16)
    product = complex_mul(system_rounded, first_rounded).astype(jnp.bfloat16)
    retarded = (2.0 * first_guess - complex_mul(first_rounded, product)).astype(jnp.bfloat16)
    source = (phonon[1] + self_lesser).astype(jnp.bfloat16)
    halfway = complex_mul(retarded, source).astype(jnp.bfloat16)
    lesser = mul_adjoint(halfway, retarded).astype(jnp.bfloat16)
    return (retarded, lesser)


def sweep_energy(boundary, energy, phonon, level_all, hamilton_all, coupling_all):
    slab_count = level_all.shape[0]
    retarded_list = [None] * slab_count
    lesser_list = [None] * slab_count
    for slab_num in reversed(range(slab_count)):
        ret_block, les_block = slab_update(
            boundary,
            energy,
            level_all[slab_num],
            hamilton_all[slab_num],
            coupling_all[slab_num],
            phonon[slab_num],
        )
        retarded_list[slab_num] = ret_block
        lesser_list[slab_num] = les_block
        boundary = jnp.stack([ret_block, les_block])
    return (jnp.stack(retarded_list), jnp.stack(lesser_list), boundary)


def cycle_phonon(blocks, neighbours, mode_index, mode_strength):
    nearest = [from_behind(blocks, "kt", offset) for offset in (1, -1)]
    farther = [from_behind(blocks, "kt", offset) for offset in (2, -2)]
    kpoint = lax.axis_index("kt")
    cycle_size = lax.axis_size("kt")
    neighbour_pair = neighbours[0]
    behind = jnp.where(neighbour_pair[0] == (kpoint - 1) % cycle_size, nearest[0], farther[0])
    forward = jnp.where(neighbour_pair[1] == (kpoint + 1) % cycle_size, nearest[1], farther[1])
    mode_table = jnp.arange(mode_strength.shape[0], dtype=jnp.int32)
    strength = jnp.sum(
        jnp.where(mode_index[0][:, None] == mode_table[None, :], mode_strength[None, :], 0.0),
        axis=1,
    )
    return (strength, behind, forward)


def weigh(strength, behind, forward):
    return strength[0] * behind.astype(jnp.float32) + strength[1] * forward.astype(jnp.float32)


def starting_blocks(contact, energy_list):
    contact_block = contact[0]
    contact_float = contact_block.astype(jnp.float32)
    skew_part = jnp.stack(
        [contact_float[0] - contact_float[0].T, contact_float[1] + contact_float[1].T]
    )
    occupation = 1.0 / (1.0 + jnp.exp((energy_list - fermi_level) / thermal))
    energy_count = energy_list.shape[0]
    contact_lesser = (-occupation[:, None, None, None] * skew_part).astype(jnp.bfloat16)
    return jnp.stack(
        [jnp.broadcast_to(contact_block, (energy_count,) + contact_block.shape), contact_lesser],
        axis=1,
    )


def body(
    energies, onsite, hamiltonian, hopping, contact, previous, neighbours, mode_index, mode_strength
):
    position = lax.axis_index("slab")
    half = previous.shape[5] // 2
    halves = [
        lax.all_to_all(
            previous[:, :, :, :, :, h * half : (h + 1) * half],
            "slab",
            split_axis=1,
            concat_axis=2,
            tiled=True,
        )
        for h in range(2)
    ]
    slab_total = halves[0].shape[2]
    slab_list = [None] * slab_total
    for slab_num in reversed(range(slab_total)):
        row_list = []
        for regrouped in halves:
            strength, behind, forward = cycle_phonon(
                regrouped[:, :, slab_num : slab_num + 1], neighbours, mode_index, mode_strength
            )
            row_list.append(weigh(strength, behind[0], forward[0]))
        slab_list[slab_num] = jnp.concatenate(row_list, axis=4)
    phonon_all = jnp.concatenate(slab_list, axis=1)
    level_whole = lax.all_gather(onsite, "slab", axis=1, tiled=True)
    hamilton_whole, coupling_whole = (
        lax.all_gather(hamiltonian, "slab", axis=1, tiled=True),
        lax.all_gather(hopping, "slab", axis=1, tiled=True),
    )
    local_count = phonon_all.shape[0]
    local_energies = lax.dynamic_slice_in_dim(energies, position * local_count, local_count, 0)
    initial = starting_blocks(contact, local_energies)

    def run_whole(boundary, energy, phonon):
        return sweep_energy(
            boundary, energy, phonon, level_whole[0], hamilton_whole[0], coupling_whole[0]
        )

    retarded_local, lesser_local, unused = jax.vmap(run_whole)(initial, local_energies, phonon_all)
    both_all = lax.all_to_all(
        as_sent(jnp.stack([retarded_local, lesser_local])[:, None]),
        "slab",
        split_axis=3,
        concat_axis=2,
        tiled=True,
    )
    return (both_all[0], both_all[1])


def solution(mesh):
    in_specs = (
        P(),
        P("kt", "slab", None),
        P("kt", "slab", None, None, None),
        P("kt", "slab", None, None, None),
        P("kt", None, None, None),
        P("kt", None, "slab", None, None, None, None),
        P("kt", None),
        P("kt", None),
        P(),
    )
    out_specs = (P("kt", None, "slab", None, None, None), P("kt", None, "slab", None, None, None))
    return jax.shard_map(body, mesh=mesh, in_specs=in_specs, out_specs=out_specs, check_vma=False)
```

profile of v0, /device:TPU:0, one launch (start us, length us, event | category | flops | bytes accessed | tf_op | source)
XLA Modules:
  0.0 550.2 jit_solution(13757800717214204489)
XLA Ops:
  7.2 5.2 fusion.324
  17.4 40.4 %all-to-all-done.1 = bf16[1,4,1,2,2,192,384]{6,5,4,3,2,0,1:T(8,128)(2,1)S(1)} async-done(((bf16[1,4,1,2,2,192,384]{6,5,4,3,2,0,1:T(8,128)(2,1)}), bf16[1,4,1,2,2,192,384]{6,5,4,3,2,0,1:T(8,128)(2,1)S(1)}, u32[]{:S(2)}, u32[]{:S(2)}) %all-to-all-start.1) | async-done | bytes 2359328 | tf_op jit(solution)/shard_map/all_to_all | solution.py:161
  65.8 5.4 collective-permute-start.6
  73.2 18.1 %all-to-all-done = bf16[1,4,1,2,2,192,384]{6,5,4,3,2,0,1:T(8,128)(2,1)S(1)} async-done(((bf16[1,4,1,2,2,192,384]{6,5,4,3,2,0,1:T(8,128)(2,1)}), bf16[1,4,1,2,2,192,384]{6,5,4,3,2,0,1:T(8,128)(2,1)S(1)}, u32[]{:S(2)}, u32[]{:S(2)}) %all-to-all-start) | async-done | bytes 2359328 | tf_op jit(solution)/shard_map/all_to_all | solution.py:161
  92.8 5.4 collective-permute-start.2
  100.9 10.6 %collective-permute-done.5 = bf16[1,1,1,2,2,192,384]{6,5,4,3,2,1,0:T(8,128)(2,1)} collective-permute-done((bf16[1,1,1,2,2,192,384]{6,5,4,3,2,1,0:T(8,128)(2,1)}, bf16[1,1,1,2,2,192,384]{6,5,4,3,2,1,0:T(8,128)(2,1)}, u32[]{:S(2)}, u32[]{:S(2)}) %collective-permute-start.5) | collective-permute-done | bytes 589856 | tf_op jit(solution)/shard_map/ppermute | solution.py:13
  115.4 7.8 %collective-permute-done.2 = bf16[1,1,1,2,2,192,384]{6,5,4,3,2,1,0:T(8,128)(2,1)S(1)} collective-permute-done((bf16[1,1,1,2,2,192,384]{6,5,4,3,2,1,0:T(8,128)(2,1)}, bf16[1,1,1,2,2,192,384]{6,5,4,3,2,1,0:T(8,128)(2,1)S(1)}, u32[]{:S(2)}, u32[]{:S(2)}) %collective-permute-start.2) | collective-permute-done | bytes 589856 | tf_op jit(solution)/shard_map/ppermute | solution.py:13
  123.7 12.5 %collective-permute-done.3 = bf16[1,1,1,2,2,192,384]{6,5,4,3,2,1,0:T(8,128)(2,1)S(1)} collective-permute-done((bf16[1,1,1,2,2,192,384]{6,5,4,3,2,1,0:T(8,128)(2,1)}, bf16[1,1,1,2,2,192,384]{6,5,4,3,2,1,0:T(8,128)(2,1)S(1)}, u32[]{:S(2)}, u32[]{:S(2)}) %collective-permute-start.3) | collective-permute-done | bytes 589856 | tf_op jit(solution)/shard_map/ppermute | solution.py:13
  138.9 10.5 %collective-permute-done.1 = bf16[1,1,1,2,2,192,384]{6,5,4,3,2,1,0:T(8,128)(2,1)S(1)} collective-permute-done((bf16[1,1,1,2,2,192,384]{6,5,4,3,2,1,0:T(8,128)(2,1)}, bf16[1,1,1,2,2,192,384]{6,5,4,3,2,1,0:T(8,128)(2,1)S(1)}, u32[]{:S(2)}, u32[]{:S(2)}) %collective-permute-start.1) | collective-permute-done | bytes 589856 | tf_op jit(solution)/shard_map/ppermute | solution.py:13
  153.2 7.8 %collective-permute-done.14 = bf16[1,1,1,2,2,192,384]{6,5,4,3,2,1,0:T(8,128)(2,1)S(1)} collective-permute-done((bf16[1,1,1,2,2,192,384]{6,5,4,3,2,1,0:T(8,128)(2,1)S(1)}, bf16[1,1,1,2,2,192,384]{6,5,4,3,2,1,0:T(8,128)(2,1)S(1)}, u32[]{:S(2)}, u32[]{:S(2)}) %collective-permute-start.14) | collective-permute-done | bytes 589856 | tf_op jit(solution)/shard_map/ppermute | solution.py:13
  161.6 12.7 %collective-permute-done.15 = bf16[1,1,1,2,2,192,384]{6,5,4,3,2,1,0:T(8,128)(2,1)} collective-permute-done((bf16[1,1,1,2,2,192,384]{6,5,4,3,2,1,0:T(8,128)(2,1)S(1)}, bf16[1,1,1,2,2,192,384]{6,5,4,3,2,1,0:T(8,128)(2,1)}, u32[]{:S(2)}, u32[]{:S(2)}) %collective-permute-start.15) | collective-permute-done | bytes 589856 | tf_op jit(solution)/shard_map/ppermute | solution.py:13
  176.9 10.6 %collective-permute-done.13 = bf16[1,1,1,2,2,192,384]{6,5,4,3,2,1,0:T(8,128)(2,1)} collective-permute-done((bf16[1,1,1,2,2,192,384]{6,5,4,3,2,1,0:T(8,128)(2,1)S(1)}, bf16[1,1,1,2,2,192,384]{6,5,4,3,2,1,0:T(8,128)(2,1)}, u32[]{:S(2)}, u32[]{:S(2)}) %collective-permute-start.13) | collective-permute-done | bytes 589856 | tf_op jit(solution)/shard_map/ppermute | solution.py:13
  196.7 5.2 all_gather.9
  202.7 9.5 %collective-permute-done.11 = bf16[1,1,1,2,2,192,384]{6,5,4,3,2,1,0:T(8,128)(2,1)} collective-permute-done((bf16[1,1,1,2,2,192,384]{6,5,4,3,2,1,0:T(8,128)(2,1)}, bf16[1,1,1,2,2,192,384]{6,5,4,3,2,1,0:T(8,128)(2,1)}, u32[]{:S(2)}, u32[]{:S(2)}) %collective-permute-start.11) | collective-permute-done | bytes 589856 | tf_op jit(solution)/shard_map/ppermute | solution.py:13
  214.9 10.6 %collective-permute-done.9 = bf16[1,1,1,2,2,192,384]{6,5,4,3,2,1,0:T(8,128)(2,1)} collective-permute-done((bf16[1,1,1,2,2,192,384]{6,5,4,3,2,1,0:T(8,128)(2,1)}, bf16[1,1,1,2,2,192,384]{6,5,4,3,2,1,0:T(8,128)(2,1)}, u32[]{:S(2)}, u32[]{:S(2)}) %collective-permute-start.9) | collective-permute-done | bytes 589856 | tf_op jit(solution)/shard_map/ppermute | solution.py:13
  229.2 7.9 %collective-permute-done.22 = bf16[1,1,1,2,2,192,384]{6,5,4,3,2,1,0:T(8,128)(2,1)} collective-permute-done((bf16[1,1,1,2,2,192,384]{6,5,4,3,2,1,0:T(8,128)(2,1)}, bf16[1,1,1,2,2,192,384]{6,5,4,3,2,1,0:T(8,128)(2,1)}, u32[]{:S(2)}, u32[]{:S(2)}) %collective-permute-start.22) | collective-permute-done | bytes 589856 | tf_op jit(solution)/shard_map/ppermute | solution.py:13
  259.9 5.2 collective-permute-start.16
  268.4 6.7 %collective-permute-done.18 = bf16[1,1,1,2,2,192,384]{6,5,4,3,2,1,0:T(8,128)(2,1)} collective-permute-done((bf16[1,1,1,2,2,192,384]{6,5,4,3,2,1,0:T(8,128)(2,1)}, bf16[1,1,1,2,2,192,384]{6,5,4,3,2,1,0:T(8,128)(2,1)}, u32[]{:S(2)}, u32[]{:S(2)}) %collective-permute-start.18) | collective-permute-done | bytes 589856 | tf_op jit(solution)/shard_map/ppermute | solution.py:13
  275.7 12.3 %collective-permute-done.19 = bf16[1,1,1,2,2,192,384]{6,5,4,3,2,1,0:T(8,128)(2,1)} collective-permute-done((bf16[1,1,1,2,2,192,384]{6,5,4,3,2,1,0:T(8,128)(2,1)}, bf16[1,1,1,2,2,192,384]{6,5,4,3,2,1,0:T(8,128)(2,1)}, u32[]{:S(2)}, u32[]{:S(2)}) %collective-permute-start.19) | collective-permute-done | bytes 589856 | tf_op jit(solution)/shard_map/ppermute | solution.py:13
  295.7 5.7 %collective-permute-done.17 = bf16[1,1,1,2,2,192,384]{6,5,4,3,2,1,0:T(8,128)(2,1)S(1)} collective-permute-done((bf16[1,1,1,2,2,192,384]{6,5,4,3,2,1,0:T(8,128)(2,1)}, bf16[1,1,1,2,2,192,384]{6,5,4,3,2,1,0:T(8,128)(2,1)S(1)}, u32[]{:S(2)}, u32[]{:S(2)}) %collective-permute-start.17) | collective-permute-done | bytes 589856 | tf_op jit(solution)/shard_map/ppermute | solution.py:13
  304.9 8.2 %collective-permute-done.30 = bf16[1,1,1,2,2,192,384]{6,5,4,3,2,1,0:T(8,128)(2,1)S(1)} collective-permute-done((bf16[1,1,1,2,2,192,384]{6,5,4,3,2,1,0:T(8,128)(2,1)}, bf16[1,1,1,2,2,192,384]{6,5,4,3,2,1,0:T(8,128)(2,1)S(1)}, u32[]{:S(2)}, u32[]{:S(2)}) %collective-permute-start.30) | collective-permute-done | bytes 589856 | tf_op jit(solution)/shard_map/ppermute | solution.py:13
  313.7 12.1 %collective-permute-done.31 = bf16[1,1,1,2,2,192,384]{6,5,4,3,2,1,0:T(8,128)(2,1)S(1)} collective-permute-done((bf16[1,1,1,2,2,192,384]{6,5,4,3,2,1,0:T(8,128)(2,1)}, bf16[1,1,1,2,2,192,384]{6,5,4,3,2,1,0:T(8,128)(2,1)S(1)}, u32[]{:S(2)}, u32[]{:S(2)}) %collective-permute-start.31) | collective-permute-done | bytes 589856 | tf_op jit(solution)/shard_map/ppermute | solution.py:13
  339.7 4.4 add_bitcast_fusion.5
  477.9 56.5 %all_to_all.33 = bf16[2,1,1,4,2,384,384]{5,6,4,0,2,1,3:T(8,128)(2,1)S(1)} all-to-all(bf16[2,1,1,4,2,384,384]{5,6,4,0,2,1,3:T(8,128)(2,1)S(1)} %copy.339), channel_id=1, replica_groups=mesh['slab'=4,'kt'=8] {'slab'}, dimensions={3} | all-to-all | bytes 9437184 | tf_op jit(solution)/shard_map/all_to_all | solution.py:196
  (421 shorter events, 241.6 us)
Async XLA Ops:
  12.4 45.4 %all-to-all-start.1 = ((bf16[1,4,1,2,2,192,384]{6,5,4,3,2,0,1:T(8,128)(2,1)}), bf16[1,4,1,2,2,192,384]{6,5,4,3,2,0,1:T(8,128)(2,1)S(1)}, u32[]{:S(2)}, u32[]{:S(2)}) async-start(bf16[1,4,1,2,2,192,384]{6,5,4,3,2,0,1:T(8,128)(2,1)} %get-tuple-element.57), calls=%async_computation.1 | async-start | bytes 4718592 | tf_op jit(solution)/shard_map/all_to_all | solution.py:161
  16.6 376.3 %all-gather.5.cloned.1.call-start = ((), (), s32[]{:S(2)}) async-start(), calls=%async_computation.4 | async-start | bytes 2949120 | tf_op jit(solution)/shard_map/all_gather | solution.py:184
  62.8 337.6 %all-gather.3.cloned.1.call-start = ((), (), s32[]{:S(2)}) async-start(), calls=%async_computation.3 | async-start | bytes 2949120 | tf_op jit(solution)/shard_map/all_gather | solution.py:183
  72.2 39.2 %collective-permute-start.5 = (bf16[1,1,1,2,2,192,384]{6,5,4,3,2,1,0:T(8,128)(2,1)}, bf16[1,1,1,2,2,192,384]{6,5,4,3,2,1,0:T(8,128)(2,1)}, u32[]{:S(2)}, u32[]{:S(2)}) collective-permute-start(bf16[1,1,1,2,2,192,384]{6,5,4,3,2,1,0:T(8,128)(2,1)} %get-tuple-element.77), channel_id=1, source_target_pairs={{0,2},{1,3},{2,4},{3,5},{4,6},{5,7},{6,0},{7,1},{8,10},{9,11},{10,... | collective-permute-start | bytes 1769480 | tf_op jit(solution)/shard_map/ppermute | solution.py:13
  99.3 50.0 %collective-permute-start.1 = (bf16[1,1,1,2,2,192,384]{6,5,4,3,2,1,0:T(8,128)(2,1)}, bf16[1,1,1,2,2,192,384]{6,5,4,3,2,1,0:T(8,128)(2,1)S(1)}, u32[]{:S(2)}, u32[]{:S(2)}) collective-permute-start(bf16[1,1,1,2,2,192,384]{6,5,4,3,2,1,0:T(8,128)(2,1)} %get-tuple-element.73), channel_id=1, source_target_pairs={{0,2},{1,3},{2,4},{3,5},{4,6},{5,7},{6,0},{7,1},{8,10},{9,11},{10,... | collective-permute-start | bytes 1769480 | tf_op jit(solution)/shard_map/ppermute | solution.py:13
  111.5 49.6 %collective-permute-start.14 = (bf16[1,1,1,2,2,192,384]{6,5,4,3,2,1,0:T(8,128)(2,1)S(1)}, bf16[1,1,1,2,2,192,384]{6,5,4,3,2,1,0:T(8,128)(2,1)S(1)}, u32[]{:S(2)}, u32[]{:S(2)}) collective-permute-start(bf16[1,1,1,2,2,192,384]{6,5,4,3,2,1,0:T(8,128)(2,1)S(1)} %get-tuple-element.76), channel_id=1, source_target_pairs={{0,7},{1,0},{2,1},{3,2},{4,3},{5,4},{6,5},{7,6},{8,15},{9,8},{10,9... | collective-permute-start | bytes 1769480 | tf_op jit(solution)/shard_map/ppermute | solution.py:13
  123.2 51.1 %collective-permute-start.15 = (bf16[1,1,1,2,2,192,384]{6,5,4,3,2,1,0:T(8,128)(2,1)S(1)}, bf16[1,1,1,2,2,192,384]{6,5,4,3,2,1,0:T(8,128)(2,1)}, u32[]{:S(2)}, u32[]{:S(2)}) collective-permute-start(bf16[1,1,1,2,2,192,384]{6,5,4,3,2,1,0:T(8,128)(2,1)S(1)} %get-tuple-element.76), channel_id=1, source_target_pairs={{0,6},{1,7},{2,0},{3,1},{4,2},{5,3},{6,4},{7,5},{8,14},{9,15},{10,... | collective-permute-start | bytes 1769480 | tf_op jit(solution)/shard_map/ppermute | solution.py:13
  137.2 50.3 %collective-permute-start.13 = (bf16[1,1,1,2,2,192,384]{6,5,4,3,2,1,0:T(8,128)(2,1)S(1)}, bf16[1,1,1,2,2,192,384]{6,5,4,3,2,1,0:T(8,128)(2,1)}, u32[]{:S(2)}, u32[]{:S(2)}) collective-permute-start(bf16[1,1,1,2,2,192,384]{6,5,4,3,2,1,0:T(8,128)(2,1)S(1)} %get-tuple-element.76), channel_id=1, source_target_pairs={{0,2},{1,3},{2,4},{3,5},{4,6},{5,7},{6,0},{7,1},{8,10},{9,11},{10,... | collective-permute-start | bytes 1769480 | tf_op jit(solution)/shard_map/ppermute | solution.py:13
  149.4 52.7 %collective-permute-start.10 = (bf16[1,1,1,2,2,192,384]{6,5,4,3,2,1,0:T(8,128)(2,1)}, bf16[1,1,1,2,2,192,384]{6,5,4,3,2,1,0:T(8,128)(2,1)}, u32[]{:S(2)}, u32[]{:S(2)}) collective-permute-start(bf16[1,1,1,2,2,192,384]{6,5,4,3,2,1,0:T(8,128)(2,1)} %get-tuple-element.72), channel_id=1, source_target_pairs={{0,7},{1,0},{2,1},{3,2},{4,3},{5,4},{6,5},{7,6},{8,15},{9,8},{10,9... | collective-permute-start | bytes 1769480 | tf_op jit(solution)/shard_map/ppermute | solution.py:13
  161.1 51.1 %collective-permute-start.11 = (bf16[1,1,1,2,2,192,384]{6,5,4,3,2,1,0:T(8,128)(2,1)}, bf16[1,1,1,2,2,192,384]{6,5,4,3,2,1,0:T(8,128)(2,1)}, u32[]{:S(2)}, u32[]{:S(2)}) collective-permute-start(bf16[1,1,1,2,2,192,384]{6,5,4,3,2,1,0:T(8,128)(2,1)} %get-tuple-element.72), channel_id=1, source_target_pairs={{0,6},{1,7},{2,0},{3,1},{4,2},{5,3},{6,4},{7,5},{8,14},{9,15},{10,... | collective-permute-start | bytes 1769480 | tf_op jit(solution)/shard_map/ppermute | solution.py:13
  175.3 50.2 %collective-permute-start.9 = (bf16[1,1,1,2,2,192,384]{6,5,4,3,2,1,0:T(8,128)(2,1)}, bf16[1,1,1,2,2,192,384]{6,5,4,3,2,1,0:T(8,128)(2,1)}, u32[]{:S(2)}, u32[]{:S(2)}) collective-permute-start(bf16[1,1,1,2,2,192,384]{6,5,4,3,2,1,0:T(8,128)(2,1)} %get-tuple-element.72), channel_id=1, source_target_pairs={{0,2},{1,3},{2,4},{3,5},{4,6},{5,7},{6,0},{7,1},{8,10},{9,11},{10,... | collective-permute-start | bytes 1769480 | tf_op jit(solution)/shard_map/ppermute | solution.py:13
  187.5 49.6 %collective-permute-start.22 = (bf16[1,1,1,2,2,192,384]{6,5,4,3,2,1,0:T(8,128)(2,1)}, bf16[1,1,1,2,2,192,384]{6,5,4,3,2,1,0:T(8,128)(2,1)}, u32[]{:S(2)}, u32[]{:S(2)}) collective-permute-start(bf16[1,1,1,2,2,192,384]{6,5,4,3,2,1,0:T(8,128)(2,1)} %get-tuple-element.75), channel_id=1, source_target_pairs={{0,7},{1,0},{2,1},{3,2},{4,3},{5,4},{6,5},{7,6},{8,15},{9,8},{10,9... | collective-permute-start | bytes 1769480 | tf_op jit(solution)/shard_map/ppermute | solution.py:13
  202.0 57.9 %collective-permute-start.23 = (bf16[1,1,1,2,2,192,384]{6,5,4,3,2,1,0:T(8,128)(2,1)}, bf16[1,1,1,2,2,192,384]{6,5,4,3,2,1,0:T(8,128)(2,1)}, u32[]{:S(2)}, u32[]{:S(2)}) collective-permute-start(bf16[1,1,1,2,2,192,384]{6,5,4,3,2,1,0:T(8,128)(2,1)} %get-tuple-element.75), channel_id=1, source_target_pairs={{0,6},{1,7},{2,0},{3,1},{4,2},{5,3},{6,4},{7,5},{8,14},{9,15},{10,... | collective-permute-start | bytes 1769480 | tf_op jit(solution)/shard_map/ppermute | solution.py:13
  212.2 53.0 %collective-permute-start.20 = (bf16[1,1,1,2,2,192,384]{6,5,4,3,2,1,0:T(8,128)(2,1)}, bf16[1,1,1,2,2,192,384]{6,5,4,3,2,1,0:T(8,128)(2,1)}, u32[]{:S(2)}, u32[]{:S(2)}) collective-permute-start(bf16[1,1,1,2,2,192,384]{6,5,4,3,2,1,0:T(8,128)(2,1)} %get-tuple-element.75), channel_id=1, source_target_pairs={{0,1},{1,2},{2,3},{3,4},{4,5},{5,6},{6,7},{7,0},{8,9},{9,10},{10,1... | collective-permute-start | bytes 1769480 | tf_op jit(solution)/shard_map/ppermute | solution.py:13
  213.2 51.9 %collective-permute-start.21 = (bf16[1,1,1,2,2,192,384]{6,5,4,3,2,1,0:T(8,128)(2,1)}, bf16[1,1,1,2,2,192,384]{6,5,4,3,2,1,0:T(8,128)(2,1)}, u32[]{:S(2)}, u32[]{:S(2)}) collective-permute-start(bf16[1,1,1,2,2,192,384]{6,5,4,3,2,1,0:T(8,128)(2,1)} %get-tuple-element.75), channel_id=1, source_target_pairs={{0,2},{1,3},{2,4},{3,5},{4,6},{5,7},{6,0},{7,1},{8,10},{9,11},{10,... | collective-permute-start | bytes 1769480 | tf_op jit(solution)/shard_map/ppermute | solution.py:13
  225.5 49.6 %collective-permute-start.18 = (bf16[1,1,1,2,2,192,384]{6,5,4,3,2,1,0:T(8,128)(2,1)}, bf16[1,1,1,2,2,192,384]{6,5,4,3,2,1,0:T(8,128)(2,1)}, u32[]{:S(2)}, u32[]{:S(2)}) collective-permute-start(bf16[1,1,1,2,2,192,384]{6,5,4,3,2,1,0:T(8,128)(2,1)} %get-tuple-element.71), channel_id=1, source_target_pairs={{0,7},{1,0},{2,1},{3,2},{4,3},{5,4},{6,5},{7,6},{8,15},{9,8},{10,9... | collective-permute-start | bytes 1769480 | tf_op jit(solution)/shard_map/ppermute | solution.py:13
  237.1 50.9 %collective-permute-start.19 = (bf16[1,1,1,2,2,192,384]{6,5,4,3,2,1,0:T(8,128)(2,1)}, bf16[1,1,1,2,2,192,384]{6,5,4,3,2,1,0:T(8,128)(2,1)}, u32[]{:S(2)}, u32[]{:S(2)}) collective-permute-start(bf16[1,1,1,2,2,192,384]{6,5,4,3,2,1,0:T(8,128)(2,1)} %get-tuple-element.71), channel_id=1, source_target_pairs={{0,6},{1,7},{2,0},{3,1},{4,2},{5,3},{6,4},{7,5},{8,14},{9,15},{10,... | collective-permute-start | bytes 1769480 | tf_op jit(solution)/shard_map/ppermute | solution.py:13
  265.1 47.9 %collective-permute-start.30 = (bf16[1,1,1,2,2,192,384]{6,5,4,3,2,1,0:T(8,128)(2,1)}, bf16[1,1,1,2,2,192,384]{6,5,4,3,2,1,0:T(8,128)(2,1)S(1)}, u32[]{:S(2)}, u32[]{:S(2)}) collective-permute-start(bf16[1,1,1,2,2,192,384]{6,5,4,3,2,1,0:T(8,128)(2,1)} %get-tuple-element.74), channel_id=1, source_target_pairs={{0,7},{1,0},{2,1},{3,2},{4,3},{5,4},{6,5},{7,6},{8,15},{9,8},{10,9... | collective-permute-start | bytes 1769480 | tf_op jit(solution)/shard_map/ppermute | solution.py:13
  275.1 50.7 %collective-permute-start.31 = (bf16[1,1,1,2,2,192,384]{6,5,4,3,2,1,0:T(8,128)(2,1)}, bf16[1,1,1,2,2,192,384]{6,5,4,3,2,1,0:T(8,128)(2,1)S(1)}, u32[]{:S(2)}, u32[]{:S(2)}) collective-permute-start(bf16[1,1,1,2,2,192,384]{6,5,4,3,2,1,0:T(8,128)(2,1)} %get-tuple-element.74), channel_id=1, source_target_pairs={{0,6},{1,7},{2,0},{3,1},{4,2},{5,3},{6,4},{7,5},{8,14},{9,15},{10,... | collective-permute-start | bytes 1769480 | tf_op jit(solution)/shard_map/ppermute | solution.py:13
  294.5 71.0 %collective-permute-start.29 = (bf16[1,1,1,2,2,192,384]{6,5,4,3,2,1,0:T(8,128)(2,1)}, bf16[1,1,1,2,2,192,384]{6,5,4,3,2,1,0:T(8,128)(2,1)}, u32[]{:S(2)}, u32[]{:S(2)}) collective-permute-start(bf16[1,1,1,2,2,192,384]{6,5,4,3,2,1,0:T(8,128)(2,1)} %get-tuple-element.74), channel_id=1, source_target_pairs={{0,2},{1,3},{2,4},{3,5},{4,6},{5,7},{6,0},{7,1},{8,10},{9,11},{10,... | collective-permute-start | bytes 1769480 | tf_op jit(solution)/shard_map/ppermute | solution.py:13
  301.4 66.4 %collective-permute-start.26 = (bf16[1,1,1,2,2,192,384]{6,5,4,3,2,1,0:T(8,128)(2,1)}, bf16[1,1,1,2,2,192,384]{6,5,4,3,2,1,0:T(8,128)(2,1)}, u32[]{:S(2)}, u32[]{:S(2)}) collective-permute-start(bf16[1,1,1,2,2,192,384]{6,5,4,3,2,1,0:T(8,128)(2,1)} %get-tuple-element.70), channel_id=1, source_target_pairs={{0,7},{1,0},{2,1},{3,2},{4,3},{5,4},{6,5},{7,6},{8,15},{9,8},{10,9... | collective-permute-start | bytes 1769480 | tf_op jit(solution)/shard_map/ppermute | solution.py:13
  313.1 57.0 %collective-permute-start.27 = (bf16[1,1,1,2,2,192,384]{6,5,4,3,2,1,0:T(8,128)(2,1)}, bf16[1,1,1,2,2,192,384]{6,5,4,3,2,1,0:T(8,128)(2,1)}, u32[]{:S(2)}, u32[]{:S(2)}) collective-permute-start(bf16[1,1,1,2,2,192,384]{6,5,4,3,2,1,0:T(8,128)(2,1)} %get-tuple-element.70), channel_id=1, source_target_pairs={{0,6},{1,7},{2,0},{3,1},{4,2},{5,3},{6,4},{7,5},{8,14},{9,15},{10,... | collective-permute-start | bytes 1769480 | tf_op jit(solution)/shard_map/ppermute | solution.py:13
  325.8 46.4 %collective-permute-start.24 = (bf16[1,1,1,2,2,192,384]{6,5,4,3,2,1,0:T(8,128)(2,1)}, bf16[1,1,1,2,2,192,384]{6,5,4,3,2,1,0:T(8,128)(2,1)}, u32[]{:S(2)}, u32[]{:S(2)}) collective-permute-start(bf16[1,1,1,2,2,192,384]{6,5,4,3,2,1,0:T(8,128)(2,1)} %get-tuple-element.70), channel_id=1, source_target_pairs={{0,1},{1,2},{2,3},{3,4},{4,5},{5,6},{6,7},{7,0},{8,9},{9,10},{10,1... | collective-permute-start | bytes 1769480 | tf_op jit(solution)/shard_map/ppermute | solution.py:13
  327.1 49.8 %collective-permute-start.25 = (bf16[1,1,1,2,2,192,384]{6,5,4,3,2,1,0:T(8,128)(2,1)}, bf16[1,1,1,2,2,192,384]{6,5,4,3,2,1,0:T(8,128)(2,1)}, u32[]{:S(2)}, u32[]{:S(2)}) collective-permute-start(bf16[1,1,1,2,2,192,384]{6,5,4,3,2,1,0:T(8,128)(2,1)} %get-tuple-element.70), channel_id=1, source_target_pairs={{0,2},{1,3},{2,4},{3,5},{4,6},{5,7},{6,0},{7,1},{8,10},{9,11},{10,... | collective-permute-start | bytes 1769480 | tf_op jit(solution)/shard_map/ppermute | solution.py:13
  (111 other events, 984.6 us)
Sparse Core Ops, SparseCore 0:
  19.0 39.4 all-gather.4
  138.9 24.6 all-gather.2
where the time goes:
time: 560 us; the launch traced here: 550 us
  waiting for transfers between devices  212 us (38%)
  local copies, waits for them, and re-layouts  120 us (21%)
  starting transfers between devices  61.8 us (11%)
  blocking collectives  61.7 us (11%)
  other arithmetic  49 us (9%)
  matrix products  28.9 us (5%)
  between operations  17.4 us (3%)
    ppermute x32, waiting for transfers between devices, from_behind(): lax.ppermute(value, axis, [(i, (i + by) % peers) for i in range(peers)])  152 us
    ppermute x32, local copies, waits for them, and re-layouts, from_behind(): lax.ppermute(value, axis, [(i, (i + by) % peers) for i in range(peers)])  59.5 us
    all_to_all x2, waiting for transfers between devices, body(): lax.all_to_all(previous[:, :, :, :, :, h * half:(h + 1) * half], 'slab',...  58.5 us
    all_to_all x1, blocking collectives, body(): lax.all_to_all(as_sent(jnp.stack([retarded_local, lesser_local])[:, None]...  56.5 us
    ppermute x32, starting transfers between devices, from_behind(): lax.ppermute(value, axis, [(i, (i + by) % peers) for i in range(peers)])  53.9 us
    unnamed x209, local copies, waits for them, and re-layouts  42.5 us
    add x8, other arithmetic, weigh(): strength[0] * behind.astype(jnp.float32)  20.3 us
    dot_general x8, matrix products, mul_adjoint(): jnp.einsum('...pij,qkj->...pqik', first_op, second_op, preferred_element_...  11.4 us
  transfers between devices with their start and end apart: 36, of which 23 were waited for; matrix products, arithmetic and copies ran while one was open for 19% of the time, Pallas kernels for 0%

commit v1 on v0

--- a/solution.py
+++ b/solution.py
@@ -6,6 +6,18 @@
 broaden = 0.05
 fermi_level = 0.0
 thermal = 0.1
+
+
+def cut_along(x, dim, size):
+    shape = x.shape
+    tiles = x.reshape(*shape[:dim], size, shape[dim] // size, *shape[dim + 1 :])
+    return jnp.moveaxis(tiles, dim, 0)
+
+
+def laid_out(parts, dim):
+    parts = jnp.moveaxis(parts, 0, dim)
+    shape = parts.shape
+    return parts.reshape(*shape[:dim], shape[dim] * shape[dim + 1], *shape[dim + 2 :])
 
 
 def from_behind(value, axis, by):
@@ -193,13 +205,15 @@
         )
 
     retarded_local, lesser_local, unused = jax.vmap(run_whole)(initial, local_energies, phonon_all)
-    both_all = lax.all_to_all(
-        as_sent(jnp.stack([retarded_local, lesser_local])[:, None]),
-        "slab",
-        split_axis=3,
-        concat_axis=2,
-        tiled=True,
-    )
+    array = as_sent(jnp.stack([retarded_local, lesser_local])[:, None])
+    size_2, position_2 = (lax.axis_size("slab"), lax.axis_index("slab"))
+    blocks_2 = cut_along(array, 3, size_2)
+    outs = [blocks_2[position_2]]
+    for step in range(1, size_2):
+        sent = blocks_2[position_2 ^ step]
+        outs.append(lax.ppermute(sent, "slab", [(i_2, i_2 ^ step) for i_2 in range(size_2)]))
+    blocks_2 = jnp.stack(outs)[position_2 ^ jnp.arange(size_2)]
+    both_all = laid_out(blocks_2, 2)
     return (both_all[0], both_all[1])
 
 

time: 560 us -> 575 us (1.027)
  starting transfers between devices: 61.8 us -> 164 us
  blocking collectives: 61.7 us -> 5.18 us
  waiting for transfers between devices: 212 us -> 171 us
  local copies, waits for them, and re-layouts: 120 us -> 129 us
    ppermute x32, waiting for transfers between devices: 152 us -> 61.9 us  [from_behind(): lax.ppermute(value, axis, [(i, (i + by) % peers) for i in range(peers)])]
    ppermute x32, starting transfers between devices: 53.9 us -> 144 us  [from_behind(): lax.ppermute(value, axis, [(i, (i + by) % peers) for i in range(peers)])]
    all_to_all x1 -> x0, blocking collectives: 56.5 us -> none  [body(): lax.all_to_all(as_sent(jnp.stack([retarded_local, lesser_local])[:, None]...]
    ppermute x0 -> x3, waiting for transfers between devices: none -> 49.7 us  [body(): lax.ppermute(sent, 'slab', [(i_2, i_2 ^ step) for i_2 in range(size_2)])]
    ppermute x0 -> x3, starting transfers between devices: none -> 11.8 us  [body(): lax.ppermute(sent, 'slab', [(i_2, i_2 ^ step) for i_2 in range(size_2)])]
    gather x0 -> x1, local copies, waits for them, and re-layouts: none -> 5.78 us  [body(): blocks_2 = jnp.stack(outs)[position_2 ^ jnp.arange(size_2)]]
    unnamed x209 -> x216, local copies, waits for them, and re-layouts: 42.5 us -> 42.5 us
  transfers between devices with their start and end apart: 36 -> 39, of which waited for: 23 -> 15; matrix products, arithmetic and copies ran while one was open for 19% -> 19% of each run, Pallas kernels for 0% -> 0%
where the time goes in v1:
time: 575 us; the launch traced here: 565 us
  waiting for transfers between devices  171 us (30%)
  starting transfers between devices  164 us (29%)
  local copies, waits for them, and re-layouts  129 us (22%)
  other arithmetic  52.3 us (9%)
  matrix products  26.4 us (5%)
  between operations  17.5 us (3%)
    ppermute x32, starting transfers between devices, from_behind(): lax.ppermute(value, axis, [(i, (i + by) % peers) for i in range(peers)])  144 us
    ppermute x32, waiting for transfers between devices, from_behind(): lax.ppermute(value, axis, [(i, (i + by) % peers) for i in range(peers)])  61.9 us
    ppermute x32, local copies, waits for them, and re-layouts, from_behind(): lax.ppermute(value, axis, [(i, (i + by) % peers) for i in range(peers)])  59.5 us
    all_to_all x2, waiting for transfers between devices, body(): lax.all_to_all(previous[:, :, :, :, :, h * half:(h + 1) * half], 'slab',...  58.3 us
    ppermute x3, waiting for transfers between devices, body(): lax.ppermute(sent, 'slab', [(i_2, i_2 ^ step) for i_2 in range(size_2)])  49.7 us
    unnamed x216, local copies, waits for them, and re-layouts  42.5 us
    add x8, other arithmetic, weigh(): strength[0] * behind.astype(jnp.float32)  19.2 us
    ppermute x3, starting transfers between devices, body(): lax.ppermute(sent, 'slab', [(i_2, i_2 ^ step) for i_2 in range(size_2)])  11.8 us
  transfers between devices with their start and end apart: 39, of which 15 were waited for; matrix products, arithmetic and copies ran while one was open for 19% of the time, Pallas kernels for 0%

profile of v1, /device:TPU:0, one launch (start us, length us, event | category | flops | bytes accessed | tf_op | source)
XLA Modules:
  0.0 565.0 jit_solution(1886322497805391101)
XLA Ops:
  7.2 5.2 fusion.330
  12.4 4.2 all-to-all-start
  17.4 40.4 %all-to-all-done = bf16[1,4,1,2,2,192,384]{6,5,4,3,2,0,1:T(8,128)(2,1)S(1)} async-done(((bf16[1,4,1,2,2,192,384]{6,5,4,3,2,0,1:T(8,128)(2,1)}), bf16[1,4,1,2,2,192,384]{6,5,4,3,2,0,1:T(8,128)(2,1)S(1)}, u32[]{:S(2)}, u32[]{:S(2)}) %all-to-all-start) | async-done | bytes 2359328 | tf_op jit(solution)/shard_map/all_to_all | solution.py:173
  73.4 17.9 %all-to-all-done.1 = bf16[1,4,1,2,2,192,384]{6,5,4,3,2,0,1:T(8,128)(2,1)S(1)} async-done(((bf16[1,4,1,2,2,192,384]{6,5,4,3,2,0,1:T(8,128)(2,1)}), bf16[1,4,1,2,2,192,384]{6,5,4,3,2,0,1:T(8,128)(2,1)S(1)}, u32[]{:S(2)}, u32[]{:S(2)}) %all-to-all-start.1) | async-done | bytes 2359328 | tf_op jit(solution)/shard_map/all_to_all | solution.py:173
  96.5 16.0 %collective-permute-start.6 = (bf16[1,1,1,2,2,192,384]{6,5,4,3,2,1,0:T(8,128)(2,1)}, bf16[1,1,1,2,2,192,384]{6,5,4,3,2,1,0:T(8,128)(2,1)S(1)}, u32[]{:S(2)}, u32[]{:S(2)}) collective-permute-start(bf16[1,1,1,2,2,192,384]{6,5,4,3,2,1,0:T(8,128)(2,1)} %get-tuple-element.85), channel_id=1, source_target_pairs={{0,7},{1,0},{2,1},{3,2},{4,3},{5,4},{6,5},{7,6},{8,15},{9,8},{10,9... | collective-permute-start | bytes 1769480 | tf_op jit(solution)/shard_map/ppermute | solution.py:25
  114.5 9.3 %collective-permute-done.4 = bf16[1,1,1,2,2,192,384]{6,5,4,3,2,1,0:T(8,128)(2,1)S(1)} collective-permute-done((bf16[1,1,1,2,2,192,384]{6,5,4,3,2,1,0:T(8,128)(2,1)}, bf16[1,1,1,2,2,192,384]{6,5,4,3,2,1,0:T(8,128)(2,1)S(1)}, u32[]{:S(2)}, u32[]{:S(2)}) %collective-permute-start.4) | collective-permute-done | bytes 589856 | tf_op jit(solution)/shard_map/ppermute | solution.py:25
  124.5 25.7 %collective-permute-start.14 = (bf16[1,1,1,2,2,192,384]{6,5,4,3,2,1,0:T(8,128)(2,1)S(1)}, bf16[1,1,1,2,2,192,384]{6,5,4,3,2,1,0:T(8,128)(2,1)}, u32[]{:S(2)}, u32[]{:S(2)}) collective-permute-start(bf16[1,1,1,2,2,192,384]{6,5,4,3,2,1,0:T(8,128)(2,1)S(1)} %get-tuple-element.84), channel_id=1, source_target_pairs={{0,7},{1,0},{2,1},{3,2},{4,3},{5,4},{6,5},{7,6},{8,15},{9,8},{10,9... | collective-permute-start | bytes 1769480 | tf_op jit(solution)/shard_map/ppermute | solution.py:25
  152.4 9.4 %collective-permute-done.12 = bf16[1,1,1,2,2,192,384]{6,5,4,3,2,1,0:T(8,128)(2,1)S(1)} collective-permute-done((bf16[1,1,1,2,2,192,384]{6,5,4,3,2,1,0:T(8,128)(2,1)S(1)}, bf16[1,1,1,2,2,192,384]{6,5,4,3,2,1,0:T(8,128)(2,1)S(1)}, u32[]{:S(2)}, u32[]{:S(2)}) %collective-permute-start.12) | collective-permute-done | bytes 589856 | tf_op jit(solution)/shard_map/ppermute | solution.py:25
  162.6 25.6 %collective-permute-start.10 = (bf16[1,1,1,2,2,192,384]{6,5,4,3,2,1,0:T(8,128)(2,1)}, bf16[1,1,1,2,2,192,384]{6,5,4,3,2,1,0:T(8,128)(2,1)}, u32[]{:S(2)}, u32[]{:S(2)}) collective-permute-start(bf16[1,1,1,2,2,192,384]{6,5,4,3,2,1,0:T(8,128)(2,1)} %get-tuple-element.80), channel_id=1, source_target_pairs={{0,7},{1,0},{2,1},{3,2},{4,3},{5,4},{6,5},{7,6},{8,15},{9,8},{10,9... | collective-permute-start | bytes 1769480 | tf_op jit(solution)/shard_map/ppermute | solution.py:25
  195.4 5.2 all_gather.9
  201.6 24.5 %collective-permute-start.22 = (bf16[1,1,1,2,2,192,384]{6,5,4,3,2,1,0:T(8,128)(2,1)}, bf16[1,1,1,2,2,192,384]{6,5,4,3,2,1,0:T(8,128)(2,1)}, u32[]{:S(2)}, u32[]{:S(2)}) collective-permute-start(bf16[1,1,1,2,2,192,384]{6,5,4,3,2,1,0:T(8,128)(2,1)} %get-tuple-element.83), channel_id=1, source_target_pairs={{0,7},{1,0},{2,1},{3,2},{4,3},{5,4},{6,5},{7,6},{8,15},{9,8},{10,9... | collective-permute-start | bytes 1769480 | tf_op jit(solution)/shard_map/ppermute | solution.py:25
  226.7 11.0 %collective-permute-done.20 = bf16[1,1,1,2,2,192,384]{6,5,4,3,2,1,0:T(8,128)(2,1)} collective-permute-done((bf16[1,1,1,2,2,192,384]{6,5,4,3,2,1,0:T(8,128)(2,1)}, bf16[1,1,1,2,2,192,384]{6,5,4,3,2,1,0:T(8,128)(2,1)}, u32[]{:S(2)}, u32[]{:S(2)}) %collective-permute-start.20) | collective-permute-done | bytes 589856 | tf_op jit(solution)/shard_map/ppermute | solution.py:25
  260.1 4.0 collective-permute-start.18
  265.9 9.9 %collective-permute-done.16 = bf16[1,1,1,2,2,192,384]{6,5,4,3,2,1,0:T(8,128)(2,1)} collective-permute-done((bf16[1,1,1,2,2,192,384]{6,5,4,3,2,1,0:T(8,128)(2,1)}, bf16[1,1,1,2,2,192,384]{6,5,4,3,2,1,0:T(8,128)(2,1)}, u32[]{:S(2)}, u32[]{:S(2)}) %collective-permute-start.16) | collective-permute-done | bytes 589856 | tf_op jit(solution)/shard_map/ppermute | solution.py:25
  276.7 13.8 %collective-permute-start.30 = (bf16[1,1,1,2,2,192,384]{6,5,4,3,2,1,0:T(8,128)(2,1)}, bf16[1,1,1,2,2,192,384]{6,5,4,3,2,1,0:T(8,128)(2,1)S(1)}, u32[]{:S(2)}, u32[]{:S(2)}) collective-permute-start(bf16[1,1,1,2,2,192,384]{6,5,4,3,2,1,0:T(8,128)(2,1)} %get-tuple-element.82), channel_id=1, source_target_pairs={{0,7},{1,0},{2,1},{3,2},{4,3},{5,4},{6,5},{7,6},{8,15},{9,8},{10,9... | collective-permute-start | bytes 1769480 | tf_op jit(solution)/shard_map/ppermute | solution.py:25
  297.0 4.6 collective-permute-done.19
  301.6 12.0 %collective-permute-done.28 = bf16[1,1,1,2,2,192,384]{6,5,4,3,2,1,0:T(8,128)(2,1)S(1)} collective-permute-done((bf16[1,1,1,2,2,192,384]{6,5,4,3,2,1,0:T(8,128)(2,1)}, bf16[1,1,1,2,2,192,384]{6,5,4,3,2,1,0:T(8,128)(2,1)S(1)}, u32[]{:S(2)}, u32[]{:S(2)}) %collective-permute-start.28) | collective-permute-done | bytes 589856 | tf_op jit(solution)/shard_map/ppermute | solution.py:25
  314.6 13.7 %collective-permute-start.26 = (bf16[1,1,1,2,2,192,384]{6,5,4,3,2,1,0:T(8,128)(2,1)}, bf16[1,1,1,2,2,192,384]{6,5,4,3,2,1,0:T(8,128)(2,1)}, u32[]{:S(2)}, u32[]{:S(2)}) collective-permute-start(bf16[1,1,1,2,2,192,384]{6,5,4,3,2,1,0:T(8,128)(2,1)} %get-tuple-element.78), channel_id=1, source_target_pairs={{0,7},{1,0},{2,1},{3,2},{4,3},{5,4},{6,5},{7,6},{8,15},{9,8},{10,9... | collective-permute-start | bytes 1769480 | tf_op jit(solution)/shard_map/ppermute | solution.py:25
  339.7 4.3 add_bitcast_fusion.5
  479.6 11.6 %collective-permute-start.33 = (bf16[2,1,1,1,2,384,384]{6,5,4,0,3,2,1:T(8,128)(2,1)}, bf16[2,1,1,1,2,384,384]{6,5,4,0,3,2,1:T(8,128)(2,1)S(1)}, u32[]{:S(2)}, u32[]{:S(2)}) collective-permute-start(bf16[2,1,1,1,2,384,384]{6,5,4,0,3,2,1:T(8,128)(2,1)} %bitcast.1000), channel_id=1, source_target_pairs={{0,16},{8,24},{16,0},{24,8},{1,17},{9,25},{17,1},{25,9},{2,18},{10... | collective-permute-start | bytes 3538952 | tf_op jit(solution)/shard_map/ppermute | solution.py:214
  493.6 24.7 %collective-permute-done.33 = bf16[2,1,1,1,2,384,384]{6,5,4,0,3,2,1:T(8,128)(2,1)S(1)} collective-permute-done((bf16[2,1,1,1,2,384,384]{6,5,4,0,3,2,1:T(8,128)(2,1)}, bf16[2,1,1,1,2,384,384]{6,5,4,0,3,2,1:T(8,128)(2,1)S(1)}, u32[]{:S(2)}, u32[]{:S(2)}) %collective-permute-start.33) | collective-permute-done | bytes 1179680 | tf_op jit(solution)/shard_map/ppermute | solution.py:214
  518.2 25.0 %collective-permute-done.34 = bf16[2,1,1,1,2,384,384]{6,5,4,0,3,2,1:T(8,128)(2,1)} collective-permute-done((bf16[2,1,1,1,2,384,384]{6,5,4,0,3,2,1:T(8,128)(2,1)}, bf16[2,1,1,1,2,384,384]{6,5,4,0,3,2,1:T(8,128)(2,1)}, u32[]{:S(2)}, u32[]{:S(2)}) %collective-permute-start.34) | collective-permute-done | bytes 1179680 | tf_op jit(solution)/shard_map/ppermute | solution.py:214
  547.0 5.8 %gather_fusion = bf16[4,2,2,384,384]{4,3,2,1,0:T(8,128)(2,1)} fusion(bf16[4,2,2,384,384]{4,3,2,1,0:T(8,128)(2,1)} %maximum_bitcast_fusion, s32[1024]{0:T(1024)S(1)} %pad_clamp_fusion), kind=kCustom, calls=%fused_computation | custom fusion | bytes 9437200 | tf_op jit(solution)/shard_map/gather | solution.py:215
  552.8 5.2 slice_bitcast_fusion
  (439 shorter events, 218.5 us)
Async XLA Ops:
  12.4 45.4 %all-to-all-start = ((bf16[1,4,1,2,2,192,384]{6,5,4,3,2,0,1:T(8,128)(2,1)}), bf16[1,4,1,2,2,192,384]{6,5,4,3,2,0,1:T(8,128)(2,1)S(1)}, u32[]{:S(2)}, u32[]{:S(2)}) async-start(bf16[1,4,1,2,2,192,384]{6,5,4,3,2,0,1:T(8,128)(2,1)} %get-tuple-element.62), calls=%async_computation | async-start | bytes 4718592 | tf_op jit(solution)/shard_map/all_to_all | solution.py:173
  16.6 375.7 %all-gather.5.cloned.1.call-start = ((), (), s32[]{:S(2)}) async-start(), calls=%async_computation.3 | async-start | bytes 2949120 | tf_op jit(solution)/shard_map/all_gather | solution.py:196
  62.8 337.0 %all-gather.3.cloned.1.call-start = ((), (), s32[]{:S(2)}) async-start(), calls=%async_computation.2 | async-start | bytes 2949120 | tf_op jit(solution)/shard_map/all_gather | solution.py:195
  69.9 42.6 %collective-permute-start.2 = (bf16[1,1,1,2,2,192,384]{6,5,4,3,2,1,0:T(8,128)(2,1)}, bf16[1,1,1,2,2,192,384]{6,5,4,3,2,1,0:T(8,128)(2,1)}, u32[]{:S(2)}, u32[]{:S(2)}) collective-permute-start(bf16[1,1,1,2,2,192,384]{6,5,4,3,2,1,0:T(8,128)(2,1)} %get-tuple-element.81), channel_id=1, source_target_pairs={{0,7},{1,0},{2,1},{3,2},{4,3},{5,4},{6,5},{7,6},{8,15},{9,8},{10,9... | collective-permute-start | bytes 1769480 | tf_op jit(solution)/shard_map/ppermute | solution.py:25
  73.1 39.6 %collective-permute-start.3 = (bf16[1,1,1,2,2,192,384]{6,5,4,3,2,1,0:T(8,128)(2,1)}, bf16[1,1,1,2,2,192,384]{6,5,4,3,2,1,0:T(8,128)(2,1)}, u32[]{:S(2)}, u32[]{:S(2)}) collective-permute-start(bf16[1,1,1,2,2,192,384]{6,5,4,3,2,1,0:T(8,128)(2,1)} %get-tuple-element.81), channel_id=1, source_target_pairs={{0,6},{1,7},{2,0},{3,1},{4,2},{5,3},{6,4},{7,5},{8,14},{9,15},{10,... | collective-permute-start | bytes 1769480 | tf_op jit(solution)/shard_map/ppermute | solution.py:25
  96.5 53.8 %collective-permute-start.6 = (bf16[1,1,1,2,2,192,384]{6,5,4,3,2,1,0:T(8,128)(2,1)}, bf16[1,1,1,2,2,192,384]{6,5,4,3,2,1,0:T(8,128)(2,1)S(1)}, u32[]{:S(2)}, u32[]{:S(2)}) collective-permute-start(bf16[1,1,1,2,2,192,384]{6,5,4,3,2,1,0:T(8,128)(2,1)} %get-tuple-element.85), channel_id=1, source_target_pairs={{0,7},{1,0},{2,1},{3,2},{4,3},{5,4},{6,5},{7,6},{8,15},{9,8},{10,9... | collective-permute-start | bytes 1769480 | tf_op jit(solution)/shard_map/ppermute | solution.py:25
  112.7 49.1 %collective-permute-start.12 = (bf16[1,1,1,2,2,192,384]{6,5,4,3,2,1,0:T(8,128)(2,1)S(1)}, bf16[1,1,1,2,2,192,384]{6,5,4,3,2,1,0:T(8,128)(2,1)S(1)}, u32[]{:S(2)}, u32[]{:S(2)}) collective-permute-start(bf16[1,1,1,2,2,192,384]{6,5,4,3,2,1,0:T(8,128)(2,1)S(1)} %get-tuple-element.84), channel_id=1, source_target_pairs={{0,1},{1,2},{2,3},{3,4},{4,5},{5,6},{6,7},{7,0},{8,9},{9,10},{10,1... | collective-permute-start | bytes 1769480 | tf_op jit(solution)/shard_map/ppermute | solution.py:25
  124.5 63.7 %collective-permute-start.14 = (bf16[1,1,1,2,2,192,384]{6,5,4,3,2,1,0:T(8,128)(2,1)S(1)}, bf16[1,1,1,2,2,192,384]{6,5,4,3,2,1,0:T(8,128)(2,1)}, u32[]{:S(2)}, u32[]{:S(2)}) collective-permute-start(bf16[1,1,1,2,2,192,384]{6,5,4,3,2,1,0:T(8,128)(2,1)S(1)} %get-tuple-element.84), channel_id=1, source_target_pairs={{0,7},{1,0},{2,1},{3,2},{4,3},{5,4},{6,5},{7,6},{8,15},{9,8},{10,9... | collective-permute-start | bytes 1769480 | tf_op jit(solution)/shard_map/ppermute | solution.py:25
  151.2 49.5 %collective-permute-start.8 = (bf16[1,1,1,2,2,192,384]{6,5,4,3,2,1,0:T(8,128)(2,1)}, bf16[1,1,1,2,2,192,384]{6,5,4,3,2,1,0:T(8,128)(2,1)}, u32[]{:S(2)}, u32[]{:S(2)}) collective-permute-start(bf16[1,1,1,2,2,192,384]{6,5,4,3,2,1,0:T(8,128)(2,1)} %get-tuple-element.80), channel_id=1, source_target_pairs={{0,1},{1,2},{2,3},{3,4},{4,5},{5,6},{6,7},{7,0},{8,9},{9,10},{10,1... | collective-permute-start | bytes 1769480 | tf_op jit(solution)/shard_map/ppermute | solution.py:25
  161.8 39.9 %collective-permute-start.9 = (bf16[1,1,1,2,2,192,384]{6,5,4,3,2,1,0:T(8,128)(2,1)}, bf16[1,1,1,2,2,192,384]{6,5,4,3,2,1,0:T(8,128)(2,1)}, u32[]{:S(2)}, u32[]{:S(2)}) collective-permute-start(bf16[1,1,1,2,2,192,384]{6,5,4,3,2,1,0:T(8,128)(2,1)} %get-tuple-element.80), channel_id=1, source_target_pairs={{0,2},{1,3},{2,4},{3,5},{4,6},{5,7},{6,0},{7,1},{8,10},{9,11},{10,... | collective-permute-start | bytes 1769480 | tf_op jit(solution)/shard_map/ppermute | solution.py:25
  162.6 63.5 %collective-permute-start.10 = (bf16[1,1,1,2,2,192,384]{6,5,4,3,2,1,0:T(8,128)(2,1)}, bf16[1,1,1,2,2,192,384]{6,5,4,3,2,1,0:T(8,128)(2,1)}, u32[]{:S(2)}, u32[]{:S(2)}) collective-permute-start(bf16[1,1,1,2,2,192,384]{6,5,4,3,2,1,0:T(8,128)(2,1)} %get-tuple-element.80), channel_id=1, source_target_pairs={{0,7},{1,0},{2,1},{3,2},{4,3},{5,4},{6,5},{7,6},{8,15},{9,8},{10,9... | collective-permute-start | bytes 1769480 | tf_op jit(solution)/shard_map/ppermute | solution.py:25
  188.3 49.5 %collective-permute-start.20 = (bf16[1,1,1,2,2,192,384]{6,5,4,3,2,1,0:T(8,128)(2,1)}, bf16[1,1,1,2,2,192,384]{6,5,4,3,2,1,0:T(8,128)(2,1)}, u32[]{:S(2)}, u32[]{:S(2)}) collective-permute-start(bf16[1,1,1,2,2,192,384]{6,5,4,3,2,1,0:T(8,128)(2,1)} %get-tuple-element.83), channel_id=1, source_target_pairs={{0,1},{1,2},{2,3},{3,4},{4,5},{5,6},{6,7},{7,0},{8,9},{9,10},{10,1... | collective-permute-start | bytes 1769480 | tf_op jit(solution)/shard_map/ppermute | solution.py:25
  200.7 59.3 %collective-permute-start.21 = (bf16[1,1,1,2,2,192,384]{6,5,4,3,2,1,0:T(8,128)(2,1)}, bf16[1,1,1,2,2,192,384]{6,5,4,3,2,1,0:T(8,128)(2,1)}, u32[]{:S(2)}, u32[]{:S(2)}) collective-permute-start(bf16[1,1,1,2,2,192,384]{6,5,4,3,2,1,0:T(8,128)(2,1)} %get-tuple-element.83), channel_id=1, source_target_pairs={{0,2},{1,3},{2,4},{3,5},{4,6},{5,7},{6,0},{7,1},{8,10},{9,11},{10,... | collective-permute-start | bytes 1769480 | tf_op jit(solution)/shard_map/ppermute | solution.py:25
  201.6 62.5 %collective-permute-start.22 = (bf16[1,1,1,2,2,192,384]{6,5,4,3,2,1,0:T(8,128)(2,1)}, bf16[1,1,1,2,2,192,384]{6,5,4,3,2,1,0:T(8,128)(2,1)}, u32[]{:S(2)}, u32[]{:S(2)}) collective-permute-start(bf16[1,1,1,2,2,192,384]{6,5,4,3,2,1,0:T(8,128)(2,1)} %get-tuple-element.83), channel_id=1, source_target_pairs={{0,7},{1,0},{2,1},{3,2},{4,3},{5,4},{6,5},{7,6},{8,15},{9,8},{10,9... | collective-permute-start | bytes 1769480 | tf_op jit(solution)/shard_map/ppermute | solution.py:25
  226.2 49.6 %collective-permute-start.16 = (bf16[1,1,1,2,2,192,384]{6,5,4,3,2,1,0:T(8,128)(2,1)}, bf16[1,1,1,2,2,192,384]{6,5,4,3,2,1,0:T(8,128)(2,1)}, u32[]{:S(2)}, u32[]{:S(2)}) collective-permute-start(bf16[1,1,1,2,2,192,384]{6,5,4,3,2,1,0:T(8,128)(2,1)} %get-tuple-element.79), channel_id=1, source_target_pairs={{0,1},{1,2},{2,3},{3,4},{4,5},{5,6},{6,7},{7,0},{8,9},{9,10},{10,1... | collective-permute-start | bytes 1769480 | tf_op jit(solution)/shard_map/ppermute | solution.py:25
  237.8 38.9 %collective-permute-start.17 = (bf16[1,1,1,2,2,192,384]{6,5,4,3,2,1,0:T(8,128)(2,1)}, bf16[1,1,1,2,2,192,384]{6,5,4,3,2,1,0:T(8,128)(2,1)}, u32[]{:S(2)}, u32[]{:S(2)}) collective-permute-start(bf16[1,1,1,2,2,192,384]{6,5,4,3,2,1,0:T(8,128)(2,1)} %get-tuple-element.79), channel_id=1, source_target_pairs={{0,2},{1,3},{2,4},{3,5},{4,6},{5,7},{6,0},{7,1},{8,10},{9,11},{10,... | collective-permute-start | bytes 1769480 | tf_op jit(solution)/shard_map/ppermute | solution.py:25
  264.1 49.5 %collective-permute-start.28 = (bf16[1,1,1,2,2,192,384]{6,5,4,3,2,1,0:T(8,128)(2,1)}, bf16[1,1,1,2,2,192,384]{6,5,4,3,2,1,0:T(8,128)(2,1)S(1)}, u32[]{:S(2)}, u32[]{:S(2)}) collective-permute-start(bf16[1,1,1,2,2,192,384]{6,5,4,3,2,1,0:T(8,128)(2,1)} %get-tuple-element.82), channel_id=1, source_target_pairs={{0,1},{1,2},{2,3},{3,4},{4,5},{5,6},{6,7},{7,0},{8,9},{9,10},{10,1... | collective-permute-start | bytes 1769480 | tf_op jit(solution)/shard_map/ppermute | solution.py:25
  276.7 51.6 %collective-permute-start.30 = (bf16[1,1,1,2,2,192,384]{6,5,4,3,2,1,0:T(8,128)(2,1)}, bf16[1,1,1,2,2,192,384]{6,5,4,3,2,1,0:T(8,128)(2,1)S(1)}, u32[]{:S(2)}, u32[]{:S(2)}) collective-permute-start(bf16[1,1,1,2,2,192,384]{6,5,4,3,2,1,0:T(8,128)(2,1)} %get-tuple-element.82), channel_id=1, source_target_pairs={{0,7},{1,0},{2,1},{3,2},{4,3},{5,4},{6,5},{7,6},{8,15},{9,8},{10,9... | collective-permute-start | bytes 1769480 | tf_op jit(solution)/shard_map/ppermute | solution.py:25
  296.7 68.7 %collective-permute-start.31 = (bf16[1,1,1,2,2,192,384]{6,5,4,3,2,1,0:T(8,128)(2,1)}, bf16[1,1,1,2,2,192,384]{6,5,4,3,2,1,0:T(8,128)(2,1)}, u32[]{:S(2)}, u32[]{:S(2)}) collective-permute-start(bf16[1,1,1,2,2,192,384]{6,5,4,3,2,1,0:T(8,128)(2,1)} %get-tuple-element.82), channel_id=1, source_target_pairs={{0,6},{1,7},{2,0},{3,1},{4,2},{5,3},{6,4},{7,5},{8,14},{9,15},{10,... | collective-permute-start | bytes 1769480 | tf_op jit(solution)/shard_map/ppermute | solution.py:25
  301.6 66.0 %collective-permute-start.24 = (bf16[1,1,1,2,2,192,384]{6,5,4,3,2,1,0:T(8,128)(2,1)}, bf16[1,1,1,2,2,192,384]{6,5,4,3,2,1,0:T(8,128)(2,1)}, u32[]{:S(2)}, u32[]{:S(2)}) collective-permute-start(bf16[1,1,1,2,2,192,384]{6,5,4,3,2,1,0:T(8,128)(2,1)} %get-tuple-element.78), channel_id=1, source_target_pairs={{0,1},{1,2},{2,3},{3,4},{4,5},{5,6},{6,7},{7,0},{8,9},{9,10},{10,1... | collective-permute-start | bytes 1769480 | tf_op jit(solution)/shard_map/ppermute | solution.py:25
  313.6 56.2 %collective-permute-start.25 = (bf16[1,1,1,2,2,192,384]{6,5,4,3,2,1,0:T(8,128)(2,1)}, bf16[1,1,1,2,2,192,384]{6,5,4,3,2,1,0:T(8,128)(2,1)}, u32[]{:S(2)}, u32[]{:S(2)}) collective-permute-start(bf16[1,1,1,2,2,192,384]{6,5,4,3,2,1,0:T(8,128)(2,1)} %get-tuple-element.78), channel_id=1, source_target_pairs={{0,2},{1,3},{2,4},{3,5},{4,6},{5,7},{6,0},{7,1},{8,10},{9,11},{10,... | collective-permute-start | bytes 1769480 | tf_op jit(solution)/shard_map/ppermute | solution.py:25
  314.6 57.5 %collective-permute-start.26 = (bf16[1,1,1,2,2,192,384]{6,5,4,3,2,1,0:T(8,128)(2,1)}, bf16[1,1,1,2,2,192,384]{6,5,4,3,2,1,0:T(8,128)(2,1)}, u32[]{:S(2)}, u32[]{:S(2)}) collective-permute-start(bf16[1,1,1,2,2,192,384]{6,5,4,3,2,1,0:T(8,128)(2,1)} %get-tuple-element.78), channel_id=1, source_target_pairs={{0,7},{1,0},{2,1},{3,2},{4,3},{5,4},{6,5},{7,6},{8,15},{9,8},{10,9... | collective-permute-start | bytes 1769480 | tf_op jit(solution)/shard_map/ppermute | solution.py:25
  328.3 48.6 %collective-permute-start.27 = (bf16[1,1,1,2,2,192,384]{6,5,4,3,2,1,0:T(8,128)(2,1)}, bf16[1,1,1,2,2,192,384]{6,5,4,3,2,1,0:T(8,128)(2,1)}, u32[]{:S(2)}, u32[]{:S(2)}) collective-permute-start(bf16[1,1,1,2,2,192,384]{6,5,4,3,2,1,0:T(8,128)(2,1)} %get-tuple-element.78), channel_id=1, source_target_pairs={{0,6},{1,7},{2,0},{3,1},{4,2},{5,3},{6,4},{7,5},{8,14},{9,15},{10,... | collective-permute-start | bytes 1769480 | tf_op jit(solution)/shard_map/ppermute | solution.py:25
  492.6 50.6 %collective-permute-start.34 = (bf16[2,1,1,1,2,384,384]{6,5,4,0,3,2,1:T(8,128)(2,1)}, bf16[2,1,1,1,2,384,384]{6,5,4,0,3,2,1:T(8,128)(2,1)}, u32[]{:S(2)}, u32[]{:S(2)}) collective-permute-start(bf16[2,1,1,1,2,384,384]{6,5,4,0,3,2,1:T(8,128)(2,1)} %bitcast.1001), channel_id=1, source_target_pairs={{0,24},{8,16},{16,8},{24,0},{1,25},{9,17},{17,9},{25,1},{2,26},{10... | collective-permute-start | bytes 3538952 | tf_op jit(solution)/shard_map/ppermute | solution.py:214
  (118 other events, 1122.3 us)
Sparse Core Ops, SparseCore 0:
  19.0 39.4 all-gather.4
  151.2 23.0 all-gather.2
